TPU v7x, 256 devices: a whole 4x4x8 slice. The times are simulated.
256 devices in a mesh: band: 32 (over y, z), chan: 8 (over x, core).
Axes of the slice: x: 4, y: 4, z: 8, core: 2. Of those that a mesh axis runs over, the one named last changes fastest.
Arguments:
- new_frames: bfloat16 [4, 128, 512, 320], P(None, 'band', 'chan'), may hold values from -6 to 6
- cached_frames: bfloat16 [2, 128, 512, 320], P(None, 'band', 'chan'), may hold values from -6 to 6
- conv_weight: bfloat16 [3, 3, 3, 512, 512], P(None, None, None, 'chan'), may hold values from -0.0546875 to 0.0546875
- out_bias: float32 [512], P('chan'), may hold values from -3 to 3
Outputs:
- conv_out: bfloat16 [4, 128, 512, 320], P(None, 'band', 'chan')
All inputs are finite; a program needn't handle non-finite values.
Results may differ from a plain program's by a relative error of at most 0.001.
Values may be sent and summed in bfloat16 or wider, within the bound.
No kernel may reach another device: no remote copies, remote signals or barrier semaphores. Data moves between devices by JAX's collectives and lax.ppermute only.
A program may use at most 128 MiB of HBM per device.

v0:
```python
import jax
import jax.numpy as jnp
from jax import lax
from jax.sharding import PartitionSpec as P


def with_halo(block, sides, width):
    for axis, dim in sides:
        count = lax.axis_size(axis)
        forward = [(i, i + 1) for i in range(count - 1)]
        backward = [(target, source) for source, target in forward]
        low = lax.ppermute(
            lax.slice_in_dim(block, block.shape[dim] - width, None, axis=dim), axis, forward
        )
        high = lax.ppermute(lax.slice_in_dim(block, 0, width, axis=dim), axis, backward)
        block = jnp.concatenate([low, block, high], axis=dim)
    return block


def convolve(padded, kernel):
    frame_count = padded.shape[0] - 2
    row_count = padded.shape[1] - 2
    col_count = padded.shape[3] - 2
    summed = jnp.zeros((frame_count, row_count, kernel.shape[3], col_count), jnp.float32)
    for time_tap in range(3):
        for row_tap in range(3):
            window = padded[time_tap : time_tap + frame_count, row_tap : row_tap + row_count]
            products = jnp.einsum(
                "kdc,frcw->kfrdw",
                kernel[time_tap, row_tap],
                window,
                preferred_element_type=jnp.float32,
            )
            summed = (
                summed
                + products[0, :, :, :, 0:col_count]
                + products[1, :, :, :, 1 : col_count + 1]
                + products[2, :, :, :, 2 : col_count + 2]
            )
    return summed


def pad_columns(layered):
    return jnp.pad(layered, ((0, 0), (0, 0), (0, 0), (1, 1)))


def on_device(new_frames, cached_frames, conv_weight, out_bias):
    stacked = jnp.concatenate([cached_frames, new_frames], axis=0)
    rimmed = with_halo(stacked, (("band", 1),), 1)
    summed = convolve(pad_columns(lax.all_gather(rimmed, "chan", axis=2, tiled=True)), conv_weight)
    return (summed + out_bias[None, None, :, None]).astype(jnp.bfloat16)


def solution(mesh):
    in_specs = (
        P(None, "band", "chan", None),
        P(None, "band", "chan", None),
        P(None, None, None, "chan", None),
        P("chan"),
    )
    out_specs = P(None, "band", "chan", None)
    return jax.shard_map(
        on_device, mesh=mesh, in_specs=in_specs, out_specs=out_specs, check_vma=False
    )
```

profile of v0, /device:TPU:1, one launch (start us, length us, event | category | flops | bytes accessed | tf_op | source)
XLA Modules:
  0.0 180.6 jit_solution(579651613324927364)
XLA Ops:
  6.5 0.0 all-gather.2.cloned.1.call-start
  6.5 1.0 constant_dynamic-update-slice_fusion.1
  7.6 1.3 constant_dynamic-update-slice_fusion
  8.9 0.1 fusion.105
  8.9 4.4 %collective-permute-start = (bf16[6,1,64,320]{3,2,1,0:T(8,128)(2,1)S(1)}, bf16[6,1,64,320]{3,2,1,0:T(8,128)(2,1)S(1)}, u32[]{:S(2)}, u32[]{:S(2)}) collective-permute-start(bf16[6,1,64,320]{3,2,1,0:T(8,128)(2,1)S(1)} %get-tuple-element.5), channel_id=1, source_target_pairs={{0,8},{8,16},{16,24},{24,32},{32,40},{40,48},{48,56},{56,64},{64,7... | collective-permute-start | bytes 737288 | tf_op jit(solution)/shard_map/ppermute | solution.py:12
  13.3 1.3 collective-permute-start.1
  14.6 4.4 %collective-permute-done = bf16[6,1,64,320]{3,2,1,0:T(8,128)(2,1)S(1)} collective-permute-done((bf16[6,1,64,320]{3,2,1,0:T(8,128)(2,1)S(1)}, bf16[6,1,64,320]{3,2,1,0:T(8,128)(2,1)S(1)}, u32[]{:S(2)}, u32[]{:S(2)}) %collective-permute-start) | collective-permute-done | bytes 245792 | tf_op jit(solution)/shard_map/ppermute | solution.py:12
  19.0 4.2 %collective-permute-done.1 = bf16[6,1,64,320]{3,2,1,0:T(8,128)(2,1)S(1)} collective-permute-done((bf16[6,1,64,320]{3,2,1,0:T(8,128)(2,1)S(1)}, bf16[6,1,64,320]{3,2,1,0:T(8,128)(2,1)S(1)}, u32[]{:S(2)}, u32[]{:S(2)}) %collective-permute-start.1) | collective-permute-done | bytes 245792 | tf_op jit(solution)/shard_map/ppermute | solution.py:15
  23.2 1.6 pad_maximum_fusion
  24.8 0.0 all-gather.2.cloned.1.call-update
  24.8 0.0 copy-start.1
  24.8 80.6 %all-gather.2.cloned.1.call-done = bf16[6,6,512,320]{3,2,1,0:T(8,128)(2,1)} async-done(((bf16[6,6,64,320]{3,2,1,0:T(8,128)(2,1)}), bf16[6,6,512,320]{3,2,1,0:T(8,128)(2,1)}) %all-gather.2.cloned.1.call-update) | async-done | bytes 11796496 | tf_op jit(solution)/shard_map/all_gather | solution.py:50
  105.4 16.7 %copy.13 = bf16[6,6,512,320]{2,3,1,0:T(8,128)(2,1)} copy(bf16[6,6,512,320]{3,2,1,0:T(8,128)(2,1)} %all-gather.2.cloned.1.call-done) | data formatting | bytes 23592960 | tf_op jit(solution)/shard_map/all_gather | solution.py:50
  122.1 0.0 copy-done.1
  122.1 0.0 copy-start
  122.1 4.5 %fusion.42 = f32[3,4,4,64,322]{4,3,0,2,1:T(8,128)S(1)} fusion(bf16[6,6,512,320]{2,3,1,0:T(8,128)(2,1)} %copy.13, bf16[3,3,3,64,512]{4,3,2,1,0:T(8,128)(2,1)S(1)} %copy-done.1), kind=kOutput, calls=%fused_computation.32 | convolution fusion | flops 1012924416 | bytes 15949824 | tf_op jit(solution)/shard_map/kdc,frcw->kfrdw/dot_general | solution.py:28
  126.6 1.4 copy-done
  128.0 1.9 %fusion.45 = f32[3,4,4,64,322]{4,3,0,2,1:T(8,128)S(1)} fusion(bf16[6,6,512,320]{2,3,1,0:T(8,128)(2,1)S(1)} %copy-done, bf16[3,3,3,64,512]{4,3,2,1,0:T(8,128)(2,1)S(1)} %copy-done.1), kind=kOutput, calls=%fused_computation.33 | convolution fusion | flops 1012924416 | bytes 15949824 | tf_op jit(solution)/shard_map/kdc,frcw->kfrdw/dot_general | solution.py:28
  129.9 4.1 %fusion.48 = f32[3,4,4,64,322]{4,3,0,2,1:T(8,128)} fusion(bf16[6,6,512,320]{2,3,1,0:T(8,128)(2,1)S(1)} %copy-done, bf16[3,3,3,64,512]{4,3,2,1,0:T(8,128)(2,1)S(1)} %copy-done.1), kind=kOutput, calls=%fused_computation.34 | convolution fusion | flops 1012924416 | bytes 15949824 | tf_op jit(solution)/shard_map/kdc,frcw->kfrdw/dot_general | solution.py:28
  134.0 4.1 %fusion.51 = f32[3,4,4,64,322]{4,3,0,2,1:T(8,128)} fusion(bf16[6,6,512,320]{2,3,1,0:T(8,128)(2,1)S(1)} %copy-done, bf16[3,3,3,64,512]{4,3,2,1,0:T(8,128)(2,1)S(1)} %copy-done.1), kind=kOutput, calls=%fused_computation.35 | convolution fusion | flops 1012924416 | bytes 15949824 | tf_op jit(solution)/shard_map/kdc,frcw->kfrdw/dot_general | solution.py:28
  138.1 4.0 %fusion.27 = f32[3,4,4,64,322]{4,3,2,1,0:T(8,128)} fusion(bf16[6,6,512,320]{2,3,1,0:T(8,128)(2,1)S(1)} %copy-done, bf16[3,3,3,64,512]{4,3,2,1,0:T(8,128)(2,1)S(1)} %copy-done.1), kind=kOutput, calls=%fused_computation.27 | convolution fusion | flops 1012924416 | bytes 15949824 | tf_op jit(solution)/shard_map/kdc,frcw->kfrdw/dot_general | solution.py:28
  142.1 4.1 %fusion.30 = f32[3,4,4,64,322]{4,3,2,1,0:T(8,128)} fusion(bf16[6,6,512,320]{2,3,1,0:T(8,128)(2,1)S(1)} %copy-done, bf16[3,3,3,64,512]{4,3,2,1,0:T(8,128)(2,1)S(1)} %copy-done.1), kind=kOutput, calls=%fused_computation.28 | convolution fusion | flops 1012924416 | bytes 15949824 | tf_op jit(solution)/shard_map/kdc,frcw->kfrdw/dot_general | solution.py:28
  146.3 4.1 %fusion.33 = f32[3,4,4,64,322]{4,3,2,1,0:T(8,128)} fusion(bf16[6,6,512,320]{2,3,1,0:T(8,128)(2,1)S(1)} %copy-done, bf16[3,3,3,64,512]{4,3,2,1,0:T(8,128)(2,1)S(1)} %copy-done.1), kind=kOutput, calls=%fused_computation.29 | convolution fusion | flops 1012924416 | bytes 15949824 | tf_op jit(solution)/shard_map/kdc,frcw->kfrdw/dot_general | solution.py:28
  150.3 4.2 %fusion.36 = f32[3,4,4,64,322]{4,3,2,1,0:T(8,128)} fusion(bf16[6,6,512,320]{2,3,1,0:T(8,128)(2,1)S(1)} %copy-done, bf16[3,3,3,64,512]{4,3,2,1,0:T(8,128)(2,1)S(1)} %copy-done.1), kind=kOutput, calls=%fused_computation.30 | convolution fusion | flops 1012924416 | bytes 15949824 | tf_op jit(solution)/shard_map/kdc,frcw->kfrdw/dot_general | solution.py:28
  154.6 0.0 copy-start.2
  154.6 4.0 %fusion.39 = f32[3,4,4,64,322]{4,3,0,2,1:T(8,128)} fusion(bf16[6,6,512,320]{2,3,1,0:T(8,128)(2,1)S(1)} %copy-done, bf16[3,3,3,64,512]{4,3,2,1,0:T(8,128)(2,1)S(1)} %copy-done.1), kind=kOutput, calls=%fused_computation.31 | convolution fusion | flops 1012924416 | bytes 15949824 | tf_op jit(solution)/shard_map/kdc,frcw->kfrdw/dot_general | solution.py:28
  158.6 0.0 copy-done.2
  158.6 15.1 %fusion.65 = bf16[4,4,64,320]{3,2,1,0:T(8,128)(2,1)} fusion(f32[3,4,4,64,322]{4,3,2,1,0:T(8,128)} %fusion.36, f32[3,4,4,64,322]{4,3,2,1,0:T(8,128)} %fusion.33, f32[3,4,4,64,322]{4,3,2,1,0:T(8,128)} %fusion.30, f32[3,4,4,64,322]{4,3,2,1,0:T(8,128)} %fusion.27, f32[3,4,4,64,322]{4,3,0,2,1:T(8,128)} %fusion.51, f32[3,4,4,64,322]{4,3,0,2,1:T(8,128)} %fusion.48, ...), kind=kLoop, calls=%fused_computation.49 | loop fusion | flops 9175040 | bytes 36045056 | tf_op jit(solution)/shard_map/convert_element_type | solution.py:51
Async XLA Ops:
  6.5 98.8 %all-gather.2.cloned.1.call-start = ((), (), s32[]{:S(2)}) async-start(), calls=%async_computation | async-start | bytes 15925248 | tf_op jit(solution)/shard_map/all_gather | solution.py:50
  8.9 10.0 %collective-permute-start = (bf16[6,1,64,320]{3,2,1,0:T(8,128)(2,1)S(1)}, bf16[6,1,64,320]{3,2,1,0:T(8,128)(2,1)S(1)}, u32[]{:S(2)}, u32[]{:S(2)}) collective-permute-start(bf16[6,1,64,320]{3,2,1,0:T(8,128)(2,1)S(1)} %get-tuple-element.5), channel_id=1, source_target_pairs={{0,8},{8,16},{16,24},{24,32},{32,40},{40,48},{48,56},{56,64},{64,7... | collective-permute-start | bytes 737288 | tf_op jit(solution)/shard_map/ppermute | solution.py:12
  13.3 9.8 %collective-permute-start.1 = (bf16[6,1,64,320]{3,2,1,0:T(8,128)(2,1)S(1)}, bf16[6,1,64,320]{3,2,1,0:T(8,128)(2,1)S(1)}, u32[]{:S(2)}, u32[]{:S(2)}) collective-permute-start(bf16[6,1,64,320]{3,2,1,0:T(8,128)(2,1)S(1)} %get-tuple-element.6), channel_id=1, source_target_pairs={{8,0},{16,8},{24,16},{32,24},{40,32},{48,40},{56,48},{64,56},{72,6... | collective-permute-start | bytes 737288 | tf_op jit(solution)/shard_map/ppermute | solution.py:15
  24.8 97.3 %copy-start.1 = (bf16[3,3,3,64,512]{4,3,2,1,0:T(8,128)(2,1)S(1)}, bf16[3,3,3,64,512]{4,3,2,1,0:T(8,128)(2,1)}, u32[]{:S(2)}) copy-start(bf16[3,3,3,64,512]{4,3,2,1,0:T(8,128)(2,1)} %param.6) | copy-start | bytes 5308420
  122.1 5.9 %copy-start = (bf16[6,6,512,320]{2,3,1,0:T(8,128)(2,1)S(1)}, bf16[6,6,512,320]{2,3,1,0:T(8,128)(2,1)}, u32[]{:S(2)}) copy-start(bf16[6,6,512,320]{2,3,1,0:T(8,128)(2,1)} %copy.13) | copy-start | bytes 35389444
  154.6 4.0 %copy-start.2 = (f32[64]{0:T(128)S(1)}, f32[64]{0:T(128)}, u32[]{:S(2)}) copy-start(f32[64]{0:T(128)} %param.7) | copy-start | bytes 772
Sparse Core Ops, SparseCore 0:
  24.9 80.4 all-gather.1
where the time goes:
time: 181 us
  waiting for transfers between devices  89.1 us (49%)
  matrix products  35.1 us (19%)
  local copies, waits for them, and re-layouts  20.5 us (11%)
  other arithmetic  16.7 us (9%)
  between operations  13.5 us (7%)
  starting transfers between devices  5.67 us (3%)
    all_gather x1, waiting for transfers between devices, on_device(): lax.all_gather(rimmed, 'chan', axis=2, tiled=True)  80.6 us
    dot_general x9, matrix products, convolve(): jnp.einsum('kdc,frcw->kfrdw', kernel[time_tap, row_tap], window, preferre...  35.1 us
    all_gather x1, local copies, waits for them, and re-layouts, on_device(): lax.all_gather(rimmed, 'chan', axis=2, tiled=True)  16.7 us
    convert_element_type x1, other arithmetic, on_device(): return (summed + out_bias[None, None, :, None]).astype(jnp.bfloat16)  15.1 us
    ppermute x1, starting transfers between devices, with_halo(): lax.ppermute(lax.slice_in_dim(block, block.shape[dim] - width, None, axis...  4.38 us
    ppermute x1, waiting for transfers between devices, with_halo(): lax.ppermute(lax.slice_in_dim(block, block.shape[dim] - width, None, axis...  4.36 us
    ppermute x1, waiting for transfers between devices, with_halo(): lax.ppermute(lax.slice_in_dim(block, 0, width, axis=dim), axis, backward)  4.19 us
  transfers between devices with their start and end apart: 3, of which 3 were waited for; matrix products, arithmetic and copies ran while one was open for 0% of the time, Pallas kernels for 0%

commit v1 on v0

--- a/solution.py
+++ b/solution.py
@@ -47,7 +47,14 @@
 def on_device(new_frames, cached_frames, conv_weight, out_bias):
     stacked = jnp.concatenate([cached_frames, new_frames], axis=0)
     rimmed = with_halo(stacked, (("band", 1),), 1)
-    summed = convolve(pad_columns(lax.all_gather(rimmed, "chan", axis=2, tiled=True)), conv_weight)
+    summed = convolve(
+        pad_columns(
+            jnp.concatenate(
+                lax.all_to_all(jnp.stack([rimmed] * lax.axis_size("chan")), "chan", 0, 0), axis=2
+            )
+        ),
+        conv_weight,
+    )
     return (summed + out_bias[None, None, :, None]).astype(jnp.bfloat16)
 
 

time: 181 us -> 258 us (1.43); the launches traced: 181 us -> 255 us
  blocking collectives: 0 us -> 161 us
  waiting for transfers between devices: 89.1 us -> 8.55 us
  between operations: 13.5 us -> 0.23 us
  local copies, waits for them, and re-layouts: 20.5 us -> 28.8 us
    all_to_all x0 -> x1, blocking collectives: none -> 161 us  [on_device(): lax.all_to_all(jnp.stack([rimmed] * lax.axis_size('chan')), 'chan', 0, 0)]
    all_gather x1 -> x0, waiting for transfers between devices: 80.6 us -> none  [on_device(): lax.all_gather(rimmed, 'chan', axis=2, tiled=True)]
    reshape x0 -> x2, local copies, waits for them, and re-layouts: none -> 22.8 us  [on_device(): jnp.concatenate(lax.all_to_all(jnp.stack([rimmed] * lax.axis_size('chan')...]
    all_gather x1 -> x0, local copies, waits for them, and re-layouts: 16.7 us -> none  [on_device(): lax.all_gather(rimmed, 'chan', axis=2, tiled=True)]
  transfers between devices with their start and end apart: 3 -> 2, of which waited for: 3 -> 2; matrix products, arithmetic and copies ran while one was open for 0% -> 0% of each run, Pallas kernels for 0% -> 0%
where the time goes in v1:
time: 258 us; the launch traced here: 255 us
  blocking collectives  161 us (62%)
  matrix products  35.1 us (14%)
  local copies, waits for them, and re-layouts  28.8 us (11%)
  other arithmetic  15.5 us (6%)
  waiting for transfers between devices  8.55 us (3%)
  starting transfers between devices  5.67 us (2%)
    all_to_all x1, blocking collectives, on_device(): lax.all_to_all(jnp.stack([rimmed] * lax.axis_size('chan')), 'chan', 0, 0)  161 us
    dot_general x9, matrix products, convolve(): jnp.einsum('kdc,frcw->kfrdw', kernel[time_tap, row_tap], window, preferre...  35.1 us
    reshape x2, local copies, waits for them, and re-layouts, on_device(): jnp.concatenate(lax.all_to_all(jnp.stack([rimmed] * lax.axis_size('chan')...  22.8 us
    convert_element_type x1, other arithmetic, on_device(): return (summed + out_bias[None, None, :, None]).astype(jnp.bfloat16)  15.1 us
  transfers between devices with their start and end apart: 2, of which 2 were waited for; matrix products, arithmetic and copies ran while one was open for 0% of the time, Pallas kernels for 0%

profile of v1, /device:TPU:1, one launch (start us, length us, event | category | flops | bytes accessed | tf_op | source)
XLA Modules:
  0.0 254.9 jit_solution(9692253513439810647)
XLA Ops:
  0.0 1.0 constant_dynamic-update-slice_fusion.1
  1.0 1.3 constant_dynamic-update-slice_fusion
  2.3 0.1 fusion.105
  2.4 4.4 %collective-permute-start = (bf16[6,1,64,320]{3,2,1,0:T(8,128)(2,1)S(1)}, bf16[6,1,64,320]{3,2,1,0:T(8,128)(2,1)S(1)}, u32[]{:S(2)}, u32[]{:S(2)}) collective-permute-start(bf16[6,1,64,320]{3,2,1,0:T(8,128)(2,1)S(1)} %get-tuple-element.5), channel_id=1, source_target_pairs={{0,8},{8,16},{16,24},{24,32},{32,40},{40,48},{48,56},{56,64},{64,7... | collective-permute-start | bytes 737288 | tf_op jit(solution)/shard_map/ppermute | solution.py:12
  6.8 1.3 collective-permute-start.1
  8.1 4.4 %collective-permute-done = bf16[6,1,64,320]{3,2,1,0:T(8,128)(2,1)S(1)} collective-permute-done((bf16[6,1,64,320]{3,2,1,0:T(8,128)(2,1)S(1)}, bf16[6,1,64,320]{3,2,1,0:T(8,128)(2,1)S(1)}, u32[]{:S(2)}, u32[]{:S(2)}) %collective-permute-start) | collective-permute-done | bytes 245792 | tf_op jit(solution)/shard_map/ppermute | solution.py:12
  12.5 4.2 %collective-permute-done.1 = bf16[6,1,64,320]{3,2,1,0:T(8,128)(2,1)S(1)} collective-permute-done((bf16[6,1,64,320]{3,2,1,0:T(8,128)(2,1)S(1)}, bf16[6,1,64,320]{3,2,1,0:T(8,128)(2,1)S(1)}, u32[]{:S(2)}, u32[]{:S(2)}) %collective-permute-start.1) | collective-permute-done | bytes 245792 | tf_op jit(solution)/shard_map/ppermute | solution.py:15
  16.6 0.4 pad_maximum_fusion
  17.0 2.3 stack.2
  19.3 161.1 %all_to_all.5 = bf16[8,6,6,64,320]{4,3,2,1,0:T(8,128)(2,1)S(1)} all-to-all(bf16[8,6,6,64,320]{4,3,2,1,0:T(8,128)(2,1)S(1)} %stack.2), channel_id=1, replica_groups=mesh['band'=32,'chan'=8] {'chan'}, dimensions={0} | all-to-all | bytes 23592960 | tf_op jit(solution)/shard_map/all_to_all | solution.py:53
  180.4 5.9 %copy.19 = bf16[6,6,8,64,320]{4,3,2,1,0:T(8,128)(2,1)} copy(bf16[6,6,8,64,320]{4,3,1,0,2:T(8,128)(2,1)S(1)} %bitcast.218) | data formatting | bytes 23592960 | tf_op jit(solution)/shard_map/reshape | solution.py:52
  186.3 0.0 copy-start.1
  186.3 16.8 %copy.20 = bf16[6,6,512,320]{2,3,1,0:T(8,128)(2,1)} copy(bf16[6,6,512,320]{3,2,1,0:T(8,128)(2,1)} %bitcast.219) | data formatting | bytes 23592960 | tf_op jit(solution)/shard_map/reshape | solution.py:52
  203.2 0.0 copy-done.1
  203.2 0.0 copy-start
  203.2 4.5 %fusion.42 = f32[3,4,4,64,322]{4,3,0,2,1:T(8,128)S(1)} fusion(bf16[6,6,512,320]{2,3,1,0:T(8,128)(2,1)} %copy.20, bf16[3,3,3,64,512]{4,3,2,1,0:T(8,128)(2,1)S(1)} %copy-done.1), kind=kOutput, calls=%fused_computation.32 | convolution fusion | flops 1012924416 | bytes 15949824 | tf_op jit(solution)/shard_map/kdc,frcw->kfrdw/dot_general | solution.py:28
  207.7 1.4 copy-done
  209.1 1.9 fusion.45
  211.0 4.1 %fusion.48 = f32[3,4,4,64,322]{4,3,0,2,1:T(8,128)} fusion(bf16[6,6,512,320]{2,3,1,0:T(8,128)(2,1)S(1)} %copy-done, bf16[3,3,3,64,512]{4,3,2,1,0:T(8,128)(2,1)S(1)} %copy-done.1), kind=kOutput, calls=%fused_computation.34 | convolution fusion | flops 1012924416 | bytes 15949824 | tf_op jit(solution)/shard_map/kdc,frcw->kfrdw/dot_general | solution.py:28
  215.1 4.1 %fusion.51 = f32[3,4,4,64,322]{4,3,0,2,1:T(8,128)} fusion(bf16[6,6,512,320]{2,3,1,0:T(8,128)(2,1)S(1)} %copy-done, bf16[3,3,3,64,512]{4,3,2,1,0:T(8,128)(2,1)S(1)} %copy-done.1), kind=kOutput, calls=%fused_computation.35 | convolution fusion | flops 1012924416 | bytes 15949824 | tf_op jit(solution)/shard_map/kdc,frcw->kfrdw/dot_general | solution.py:28
  219.2 4.0 %fusion.27 = f32[3,4,4,64,322]{4,3,2,1,0:T(8,128)} fusion(bf16[6,6,512,320]{2,3,1,0:T(8,128)(2,1)S(1)} %copy-done, bf16[3,3,3,64,512]{4,3,2,1,0:T(8,128)(2,1)S(1)} %copy-done.1), kind=kOutput, calls=%fused_computation.27 | convolution fusion | flops 1012924416 | bytes 15949824 | tf_op jit(solution)/shard_map/kdc,frcw->kfrdw/dot_general | solution.py:28
  223.2 4.1 %fusion.30 = f32[3,4,4,64,322]{4,3,2,1,0:T(8,128)} fusion(bf16[6,6,512,320]{2,3,1,0:T(8,128)(2,1)S(1)} %copy-done, bf16[3,3,3,64,512]{4,3,2,1,0:T(8,128)(2,1)S(1)} %copy-done.1), kind=kOutput, calls=%fused_computation.28 | convolution fusion | flops 1012924416 | bytes 15949824 | tf_op jit(solution)/shard_map/kdc,frcw->kfrdw/dot_general | solution.py:28
  227.3 4.1 %fusion.33 = f32[3,4,4,64,322]{4,3,2,1,0:T(8,128)} fusion(bf16[6,6,512,320]{2,3,1,0:T(8,128)(2,1)S(1)} %copy-done, bf16[3,3,3,64,512]{4,3,2,1,0:T(8,128)(2,1)S(1)} %copy-done.1), kind=kOutput, calls=%fused_computation.29 | convolution fusion | flops 1012924416 | bytes 15949824 | tf_op jit(solution)/shard_map/kdc,frcw->kfrdw/dot_general | solution.py:28
  231.4 4.2 %fusion.36 = f32[3,4,4,64,322]{4,3,2,1,0:T(8,128)} fusion(bf16[6,6,512,320]{2,3,1,0:T(8,128)(2,1)S(1)} %copy-done, bf16[3,3,3,64,512]{4,3,2,1,0:T(8,128)(2,1)S(1)} %copy-done.1), kind=kOutput, calls=%fused_computation.30 | convolution fusion | flops 1012924416 | bytes 15949824 | tf_op jit(solution)/shard_map/kdc,frcw->kfrdw/dot_general | solution.py:28
  235.6 0.0 copy-start.2
  235.6 4.0 %fusion.39 = f32[3,4,4,64,322]{4,3,0,2,1:T(8,128)} fusion(bf16[6,6,512,320]{2,3,1,0:T(8,128)(2,1)S(1)} %copy-done, bf16[3,3,3,64,512]{4,3,2,1,0:T(8,128)(2,1)S(1)} %copy-done.1), kind=kOutput, calls=%fused_computation.31 | convolution fusion | flops 1012924416 | bytes 15949824 | tf_op jit(solution)/shard_map/kdc,frcw->kfrdw/dot_general | solution.py:28
  239.7 0.0 copy-done.2
  239.7 15.1 %fusion.65 = bf16[4,4,64,320]{3,2,1,0:T(8,128)(2,1)} fusion(f32[3,4,4,64,322]{4,3,2,1,0:T(8,128)} %fusion.36, f32[3,4,4,64,322]{4,3,2,1,0:T(8,128)} %fusion.33, f32[3,4,4,64,322]{4,3,2,1,0:T(8,128)} %fusion.30, f32[3,4,4,64,322]{4,3,2,1,0:T(8,128)} %fusion.27, f32[3,4,4,64,322]{4,3,0,2,1:T(8,128)} %fusion.51, f32[3,4,4,64,322]{4,3,0,2,1:T(8,128)} %fusion.48, ...), kind=kLoop, calls=%fused_computation.49 | loop fusion | flops 9175040 | bytes 36045056 | tf_op jit(solution)/shard_map/convert_element_type | solution.py:58
Async XLA Ops:
  2.4 10.0 %collective-permute-start = (bf16[6,1,64,320]{3,2,1,0:T(8,128)(2,1)S(1)}, bf16[6,1,64,320]{3,2,1,0:T(8,128)(2,1)S(1)}, u32[]{:S(2)}, u32[]{:S(2)}) collective-permute-start(bf16[6,1,64,320]{3,2,1,0:T(8,128)(2,1)S(1)} %get-tuple-element.5), channel_id=1, source_target_pairs={{0,8},{8,16},{16,24},{24,32},{32,40},{40,48},{48,56},{56,64},{64,7... | collective-permute-start | bytes 737288 | tf_op jit(solution)/shard_map/ppermute | solution.py:12
  6.8 9.8 %collective-permute-start.1 = (bf16[6,1,64,320]{3,2,1,0:T(8,128)(2,1)S(1)}, bf16[6,1,64,320]{3,2,1,0:T(8,128)(2,1)S(1)}, u32[]{:S(2)}, u32[]{:S(2)}) collective-permute-start(bf16[6,1,64,320]{3,2,1,0:T(8,128)(2,1)S(1)} %get-tuple-element.6), channel_id=1, source_target_pairs={{8,0},{16,8},{24,16},{32,24},{40,32},{48,40},{56,48},{64,56},{72,6... | collective-permute-start | bytes 737288 | tf_op jit(solution)/shard_map/ppermute | solution.py:15
  186.3 16.8 %copy-start.1 = (bf16[3,3,3,64,512]{4,3,2,1,0:T(8,128)(2,1)S(1)}, bf16[3,3,3,64,512]{4,3,2,1,0:T(8,128)(2,1)}, u32[]{:S(2)}) copy-start(bf16[3,3,3,64,512]{4,3,2,1,0:T(8,128)(2,1)} %param.6) | copy-start | bytes 5308420
  203.2 5.9 %copy-start = (bf16[6,6,512,320]{2,3,1,0:T(8,128)(2,1)S(1)}, bf16[6,6,512,320]{2,3,1,0:T(8,128)(2,1)}, u32[]{:S(2)}) copy-start(bf16[6,6,512,320]{2,3,1,0:T(8,128)(2,1)} %copy.20) | copy-start | bytes 35389444
  235.6 4.1 %copy-start.2 = (f32[64]{0:T(128)S(1)}, f32[64]{0:T(128)}, u32[]{:S(2)}) copy-start(f32[64]{0:T(128)} %param.7) | copy-start | bytes 772
